TPU v7x, 512 devices: a whole 4x8x8 slice. The times are simulated.
512 devices in a mesh: dp: 4 (over y_lo), head: 8 (over z), ctx: 16 (over x, y_hi, core).
Axes of the slice: x: 4, y: 8 (y_hi: 2, y_lo: 4; y = y_hi * 4 + y_lo), z: 8, core: 2. Of those that a mesh axis runs over, the one named last changes fastest.
Arguments:
- query_rows: bfloat16 [16384, 8192], P(('dp', 'ctx'), 'head'), parts along dimension 0, may hold values from -12 to 12
- key_rows: bfloat16 [16384, 1024], P(('dp', 'ctx'), 'head'), parts along dimension 0, may hold values from -4 to 4
- stored_value_rows: bfloat16 [16384, 1024], P(('dp', 'ctx'), 'head'), parts along dimension 0, may hold values from -6 to 6
- out_grad: bfloat16 [16384, 8192], P(('dp', 'ctx'), 'head'), parts along dimension 0, may hold values from -6 to 6
- block_table: int32 [64, 2], P('dp'), parts along dimension 0, may hold values from 0 to 31, as said below
- pattern: int32 [128, 10], P('dp'), parts along dimension 0, may hold values from 0 to 31, as said below
Outputs:
- attended: bfloat16 [16384, 8192], P(('dp', 'ctx'), 'head'), parts along dimension 0
- query_grad: bfloat16 [16384, 8192], P(('dp', 'ctx'), 'head'), parts along dimension 0
- key_grad: bfloat16 [16384, 1024], P(('dp', 'ctx'), 'head'), parts along dimension 0
- value_grad: bfloat16 [16384, 1024], P(('dp', 'ctx'), 'head'), parts along dimension 0
There are 4 independent parts, one for each index of `dp`. A program takes and returns all parts, laid end to end along the dimension named above; each array names one. Nothing has to cross between parts.
Inputs may be any that keep to these rules, and one draw needn't show every extreme that they name: `pattern`: row b lists the key blocks that sequence block b reads, in no order; every entry is at most b; b, max(b - 1, 0) and 0 are always listed; repeated entries count once. `block_table`: each sequence block is held by exactly one storage block, and sequence blocks b and 31 - b are held by the same ctx index.
All inputs are finite; a program needn't handle non-finite values.
Results may differ from a plain program's by a relative error of at most 0.015.
Values may be sent and summed in bfloat16 or wider, within the bound.
No kernel may reach another device: no remote copies, remote signals or barrier semaphores. Data moves between devices by JAX's collectives and lax.ppermute only.
A program may use at most 64 MiB of HBM per device.

v0:
```python
import jax
import jax.numpy as jnp
from jax import lax
from jax.sharding import PartitionSpec as P

HEAD_SIZE = 128
BLK = 128


def slot_layout(block_table, pattern, held_seq):
    blocks = pattern.shape[0]
    slots = pattern.shape[1]
    block_ids = jnp.arange(blocks, dtype=jnp.int32)
    store_seq = block_table.reshape(-1)
    inverse = jnp.sum(
        jnp.where(store_seq[:, None] == block_ids[None, :], block_ids[:, None], 0), axis=0
    )
    onehot = (held_seq[:, None] == block_ids[None, :]).astype(jnp.int32)
    held_pattern = jnp.sum(onehot[:, :, None] * pattern[None, :, :], axis=1)
    key_store = jnp.sum(
        jnp.where(held_pattern[:, :, None] == block_ids[None, None, :], inverse[None, None, :], 0),
        axis=2,
    )
    same = held_pattern[:, :, None] == held_pattern[:, None, :]
    slot_ids = jnp.arange(slots, dtype=jnp.int32)
    before = slot_ids[None, :] < slot_ids[:, None]
    live_slot = jnp.logical_not(jnp.any(same & before[None], axis=2))
    inner = jnp.arange(BLK, dtype=jnp.int32)
    query_pos = held_seq[:, None] * BLK + inner[None, :]
    key_pos = held_pattern[:, :, None] * BLK + inner[None, None, :]
    allowed = live_slot[:, None, :, None] & (key_pos[:, None, :, :] <= query_pos[:, :, None, None])
    return (key_store, allowed)


def attend_tiles(query_held, grad_held, key_tiles, value_tiles, allowed):
    scaling = HEAD_SIZE ** (-0.5)
    scores = (
        jnp.einsum("biagd,bjkad->bagijk", query_held, key_tiles, preferred_element_type=jnp.float32)
        * scaling
    )
    scores = jnp.where(allowed[:, None, None], scores, -jnp.inf)
    row_max = jnp.max(scores, axis=(4, 5), keepdims=True)
    row_sum = jnp.sum(jnp.exp(scores - row_max), axis=(4, 5), keepdims=True)
    log_total = row_max + jnp.log(row_sum)
    prob_full = jnp.exp(scores - log_total)
    prob_low = prob_full.astype(jnp.bfloat16)
    attended_wide = jnp.einsum(
        "bagijk,bjkad->biagd", prob_low, value_tiles, preferred_element_type=jnp.float32
    )
    attended = attended_wide.astype(jnp.bfloat16)
    row_dot = jnp.sum(grad_held.astype(jnp.float32) * attended_wide, axis=-1)
    row_dot = jnp.transpose(row_dot, (0, 2, 3, 1))[..., None, None]
    grad_prob = jnp.einsum(
        "biagd,bjkad->bagijk", grad_held, value_tiles, preferred_element_type=jnp.float32
    )
    grad_score = (prob_full * (grad_prob - row_dot) * scaling).astype(jnp.bfloat16)
    query_grad = jnp.einsum(
        "bagijk,bjkad->biagd", grad_score, key_tiles, preferred_element_type=jnp.float32
    ).astype(jnp.bfloat16)
    key_grads = jnp.einsum(
        "bagijk,biagd->bjkad", grad_score, query_held, preferred_element_type=jnp.float32
    )
    value_grads = jnp.einsum(
        "bagijk,biagd->bjkad", prob_low, grad_held, preferred_element_type=jnp.float32
    )
    return (attended, query_grad, key_grads, value_grads)


def per_device(query_rows, key_rows, stored_value_rows, out_grad, block_table, pattern):
    ctx_index = lax.axis_index("ctx")
    per_dev = block_table.shape[1]
    blocks = pattern.shape[0]
    kv_local = key_rows.shape[1] // HEAD_SIZE
    groups = query_rows.shape[1] // key_rows.shape[1]
    held_rows = per_dev * BLK
    held_seq = lax.dynamic_index_in_dim(block_table, ctx_index, 0, keepdims=False)
    key_store, allowed = slot_layout(block_table, pattern, held_seq)
    key_all, value_all = (
        lax.all_gather(key_rows, "ctx", axis=0, tiled=True),
        lax.all_gather(stored_value_rows, "ctx", axis=0, tiled=True),
    )
    key_blocks = key_all.reshape(blocks, BLK, kv_local, HEAD_SIZE)
    value_blocks = value_all.reshape(blocks, BLK, kv_local, HEAD_SIZE)
    key_tiles = key_blocks[key_store]
    value_tiles = value_blocks[key_store]
    query_held = query_rows.reshape(per_dev, BLK, kv_local, groups, HEAD_SIZE)
    grad_held = out_grad.reshape(per_dev, BLK, kv_local, groups, HEAD_SIZE)
    attended, query_grad, key_grads, value_grads = attend_tiles(
        query_held, grad_held, key_tiles, value_tiles, allowed
    )
    flat_slots = key_store.reshape(-1)
    key_partial = (
        jnp.zeros((blocks, BLK, kv_local, HEAD_SIZE), jnp.float32)
        .at[flat_slots]
        .add(key_grads.reshape(-1, BLK, kv_local, HEAD_SIZE))
    )
    value_partial = (
        jnp.zeros((blocks, BLK, kv_local, HEAD_SIZE), jnp.float32)
        .at[flat_slots]
        .add(value_grads.reshape(-1, BLK, kv_local, HEAD_SIZE))
    )
    key_sum, value_sum = (
        lax.psum_scatter(
            key_partial.reshape(blocks * BLK, -1).astype(jnp.bfloat16),
            "ctx",
            scatter_dimension=0,
            tiled=True,
        ).astype(jnp.float32),
        lax.psum_scatter(
            value_partial.reshape(blocks * BLK, -1).astype(jnp.bfloat16),
            "ctx",
            scatter_dimension=0,
            tiled=True,
        ).astype(jnp.float32),
    )
    attended = attended.reshape(held_rows, -1)
    query_grad = query_grad.reshape(held_rows, -1)
    key_grad = key_sum.astype(jnp.bfloat16)
    value_grad = value_sum.astype(jnp.bfloat16)
    return (attended, query_grad, key_grad, value_grad)


def solution(mesh):
    in_specs = (
        P(("dp", "ctx"), "head"),
        P(("dp", "ctx"), "head"),
        P(("dp", "ctx"), "head"),
        P(("dp", "ctx"), "head"),
        P("dp", None),
        P("dp", None),
    )
    out_specs = (
        P(("dp", "ctx"), "head"),
        P(("dp", "ctx"), "head"),
        P(("dp", "ctx"), "head"),
        P(("dp", "ctx"), "head"),
    )
    return jax.shard_map(
        per_device, mesh=mesh, in_specs=in_specs, out_specs=out_specs, check_vma=False
    )
```

profile of v0, /device:TPU:2, one launch (start us, length us, event | category | flops | bytes accessed | tf_op | source)
XLA Modules:
  0.0 322.2 jit_solution(11498761475473287322)
XLA Ops:
  12.6 1.1 copy.98
  13.8 1.1 convert_bitcast_fusion
  14.9 1.1 copy.100
  17.1 1.4 copy.65
  19.0 54.9 %all-gather.5.cloned.1.call-done = bf16[4096,128]{1,0:T(8,128)(2,1)} async-done(((bf16[256,128]{1,0:T(8,128)(2,1)}), bf16[4096,128]{1,0:T(8,128)(2,1)}) %all-gather.5.cloned.1.call-update) | async-done | bytes 1048592 | tf_op jit(solution)/shard_map/all_gather | solution.py:79
  73.9 1.9 gather_fusion.1
  75.8 1.5 fusion.4
  77.4 2.3 exponential_reduce_fusion
  79.7 2.5 fusion.9
  82.2 1.5 broadcast.134.clone.1
  83.8 5.8 %scatter_fusion.1 = f32[32,128,128]{2,1,0:T(8,128)} fusion(f32[32,128,128]{2,1,0:T(8,128)} %broadcast.134.clone.1, s32[20]{0:T(128)S(1)} %fusion.17, f32[20,128,128]{2,1,0:T(8,128)S(1)} %bitcast.169), kind=kCustom, calls=%fused_computation.3 | custom fusion | flops 327680 | bytes 3932240 | tf_op jit(solution)/shard_map/scatter-add | solution.py:100
  89.6 3.0 convert_element_type.70
  92.9 41.2 %all-gather.3.cloned.1.call-done = bf16[4096,128]{1,0:T(8,128)(2,1)} async-done(((bf16[256,128]{1,0:T(8,128)(2,1)}), bf16[4096,128]{1,0:T(8,128)(2,1)}) %all-gather.3.cloned.1.call-update) | async-done | bytes 1048592 | tf_op jit(solution)/shard_map/all_gather | solution.py:80
  134.0 2.8 gather_fusion
  136.8 8.0 %multiply_reduce_fusion = (f32[2,128,8]{1,2,0:T(8,128)S(1)}, bf16[2,128,1,8,128]{1,4,3,0,2:T(8,128)(2,1)}) fusion(f32[2,128,1,8,128]{1,4,3,0,2:T(8,128)} %copy.65, bf16[2,10,128,128,1]{3,2,4,1,0:T(8,128)(2,1)} %bitcast.170, f32[2,10,128,128,8]{3,2,4,1,0:T(8,128)} %copy-done, f32[2,8,128]{2,1,0:T(8,128)S(1)} %log_add_fusion, ...), kind=kOutput, calls=%fused_computation.21 | convolution fusion | flops 682358784 | bytes 13058048 | tf_op jit(solution)/shard_map/bagijk,bjkad->biagd/dot_general | solution.py:47
  144.8 3.6 %fusion.6 = bf16[2,8,128,10,128]{2,4,1,3,0:T(8,128)(2,1)S(1)} fusion(f32[2,10,128,128,8]{3,2,4,1,0:T(8,128)S(1)} %bitcast.157, f32[2,8,128]{2,1,0:T(8,128)S(1)} %bitcast.175, f32[2,8,128]{2,1,0:T(8,128)S(1)} %log_add_fusion, pred[2,128,10,128]{1,3,2,0:T(8,128)(4,1)S(1)} %copy-done.3, bf16[2,10,128,128,1]{3,2,4,1,0:T(8,128)(2,1)S(1)} %bitcast.171, ...), kind=kOutput, calls=%fused_computation.14 | convolution fusion | flops 689438720 | bytes 17252352 | tf_op jit(solution)/shard_map/biagd,bjkad->bagijk/dot_general | solution.py:53
  148.5 2.3 copy-done.1
  150.8 2.6 fusion.12
  153.6 4.4 %scatter_fusion = f32[32,128,128]{2,1,0:T(8,128)S(1)} fusion(f32[32,128,128]{2,1,0:T(8,128)S(1)} %broadcast.134.clone, s32[20]{0:T(128)S(1)} %fusion.17, f32[20,128,128]{2,1,0:T(8,128)} %bitcast.160), kind=kCustom, calls=%fused_computation.2 | custom fusion | flops 327680 | bytes 3932240 | tf_op jit(solution)/shard_map/scatter-add | solution.py:95
  158.1 1.2 convert_element_type.69
  159.3 3.5 %fusion.8 = bf16[2,128,1,8,128]{1,4,3,0,2:T(8,128)(2,1)S(1)} fusion(bf16[2,10,128,128,1]{3,2,4,1,0:T(8,128)(2,1)S(1)} %bitcast.159, bf16[2,8,128,10,128]{2,4,1,3,0:T(8,128)(2,1)} %copy-done.1), kind=kOutput, calls=%fused_computation.19 | convolution fusion | flops 671350784 | bytes 6422528 | tf_op jit(solution)/shard_map/bagijk,bjkad->biagd/dot_general | solution.py:57
  163.4 1.2 copy_bitcast_fusion
  164.6 60.9 %reduce-scatter.5.cloned.1.call-done = bf16[256,128]{1,0:T(8,128)(2,1)} async-done(((bf16[4096,128]{1,0:T(8,128)(2,1)}), bf16[256,128]{1,0:T(8,128)(2,1)}) %reduce-scatter.5.cloned.1.call-update) | async-done | bytes 65552 | tf_op jit(solution)/shard_map/reduce_scatter | solution.py:109
  225.5 90.2 %reduce-scatter.3.cloned.1.call-done = bf16[256,128]{1,0:T(8,128)(2,1)} async-done(((bf16[4096,128]{1,0:T(8,128)(2,1)}), bf16[256,128]{1,0:T(8,128)(2,1)}) %reduce-scatter.3.cloned.1.call-update) | async-done | bytes 65552 | tf_op jit(solution)/shard_map/reduce_scatter | solution.py:103
  (59 shorter events, 8.1 us)
Async XLA Ops:
  7.2 66.7 %all-gather.5.cloned.1.call-start = ((), (), s32[]{:S(2)}) async-start(), calls=%async_computation.3 | async-start | bytes 1114112 | tf_op jit(solution)/shard_map/all_gather | solution.py:79
  7.9 126.1 %all-gather.3.cloned.1.call-start = ((), (), s32[]{:S(2)}) async-start(), calls=%async_computation.2 | async-start | bytes 1114112 | tf_op jit(solution)/shard_map/all_gather | solution.py:80
  8.6 216.8 %reduce-scatter.5.cloned.1.call-start = ((), (), s32[]{:S(2)}) async-start(), calls=%async_computation.5 | async-start | bytes 1114112 | tf_op jit(solution)/shard_map/reduce_scatter | solution.py:109
  19.0 64.8 %copy-start.2 = (pred[2,128,10,128]{1,3,2,0:T(8,128)(4,1)}, pred[2,128,10,128]{1,3,2,0:T(8,128)(4,1)S(1)}, u32[]{:S(2)}) copy-start(pred[2,128,10,128]{1,3,2,0:T(8,128)(4,1)S(1)} %compare_and_fusion) | copy-start | bytes 983044
  75.8 3.9 %copy-start.5 = (bf16[2,128,8,128,1]{3,2,1,0,4:T(8,128)(2,1)S(1)}, bf16[2,128,8,128,1]{3,2,1,0,4:T(8,128)(2,1)}, u32[]{:S(2)}) copy-start(bf16[2,128,8,128,1]{3,2,1,0,4:T(8,128)(2,1)} %bitcast_bitcast_fusion) | copy-start | bytes 1572868
  77.4 4.9 %copy-start = (f32[2,10,128,128,8]{3,2,4,1,0:T(8,128)}, f32[2,10,128,128,8]{3,2,4,1,0:T(8,128)S(1)}, u32[]{:S(2)}) copy-start(f32[2,10,128,128,8]{3,2,4,1,0:T(8,128)S(1)} %get-tuple-element.7) | copy-start | bytes 31457284
  89.6 55.1 %slice-start = ((s8[10485760]{0:T(1024)(128)(4,1)}), s8[2097152]{0:T(1024)(128)(4,1)S(1)}, s32[]{:S(2)}) async-start(s8[10485760]{0:T(1024)(128)(4,1)} %bitcast.156), calls=%async_computation.6 | async-start | bytes 4194304
  92.6 223.0 %reduce-scatter.3.cloned.1.call-start = ((), (), s32[]{:S(2)}) async-start(), calls=%async_computation.4 | async-start | bytes 1114112 | tf_op jit(solution)/shard_map/reduce_scatter | solution.py:103
  136.8 8.0 %copy-start.3 = (pred[2,128,10,128]{1,3,2,0:T(8,128)(4,1)S(1)}, pred[2,128,10,128]{1,3,2,0:T(8,128)(4,1)}, u32[]{:S(2)}) copy-start(pred[2,128,10,128]{1,3,2,0:T(8,128)(4,1)} %copy-done.2) | copy-start | bytes 983044
  136.8 8.0 %copy-start.4 = (bf16[20,128,128]{2,1,0:T(8,128)(2,1)S(1)}, bf16[20,128,128]{2,1,0:T(8,128)(2,1)}, u32[]{:S(2)}) copy-start(bf16[20,128,128]{2,1,0:T(8,128)(2,1)} %gather_fusion) | copy-start | bytes 1966084
  136.8 8.0 %copy-start.6 = (bf16[2,128,8,128,1]{3,2,1,0,4:T(8,128)(2,1)S(1)}, bf16[2,128,8,128,1]{3,2,1,0,4:T(8,128)(2,1)}, u32[]{:S(2)}) copy-start(bf16[2,128,8,128,1]{3,2,1,0,4:T(8,128)(2,1)} %bitcast_bitcast_fusion) | copy-start | bytes 1572868
  136.8 8.0 %slice-start.1 = ((s8[10485760]{0:T(1024)(128)(4,1)}), s8[4194304]{0:T(1024)(128)(4,1)S(1)}, s32[]{:S(2)}) async-start(s8[10485760]{0:T(1024)(128)(4,1)} %bitcast.156), calls=%async_computation.7 | async-start | bytes 8388608
  136.8 8.0 %slice-start.2 = ((s8[10485760]{0:T(1024)(128)(4,1)}), s8[4194304]{0:T(1024)(128)(4,1)S(1)}, s32[]{:S(2)}) async-start(s8[10485760]{0:T(1024)(128)(4,1)} %bitcast.156), calls=%async_computation.8 | async-start | bytes 8388608
  148.5 2.3 copy-start.1
  153.4 9.7 %copy-start.7 = (bf16[2,128,1,8,128]{1,4,3,0,2:T(8,128)(2,1)S(1)}, bf16[2,128,1,8,128]{1,4,3,0,2:T(8,128)(2,1)}, u32[]{:S(2)}) copy-start(bf16[2,128,1,8,128]{1,4,3,0,2:T(8,128)(2,1)} %get-tuple-element.5) | copy-start | bytes 1572868
Sparse Core Ops, SparseCore 0:
  11.3 62.5 all-gather.4
  77.2 56.8 all-gather.2
  139.3 86.1 reduce-scatter.4
  231.3 84.2 reduce-scatter.2
where the time goes:
time: 323 us; the launch traced here: 322 us
  waiting for transfers between devices  249 us (77%)
  matrix products  21.8 us (7%)
  other arithmetic  20.2 us (6%)
  local copies, waits for them, and re-layouts  17.3 us (5%)
  between operations  14 us (4%)
    reduce_scatter x1, waiting for transfers between devices, per_device(): lax.psum_scatter(key_partial.reshape(blocks * BLK, -1).astype(jnp.bfloat1...  90.2 us
    reduce_scatter x1, waiting for transfers between devices, per_device(): lax.psum_scatter(value_partial.reshape(blocks * BLK, -1).astype(jnp.bfloa...  60.9 us
    all_gather x1, waiting for transfers between devices, per_device(): lax.all_gather(key_rows, 'ctx', axis=0, tiled=True)  54.9 us
    all_gather x1, waiting for transfers between devices, per_device(): lax.all_gather(stored_value_rows, 'ctx', axis=0, tiled=True)  41.2 us
    dot_general x1, matrix products, attend_tiles(): jnp.einsum('bagijk,bjkad->biagd', prob_low, value_tiles, preferred_elemen...  7.98 us
  transfers between devices with their start and end apart: 4, of which 4 were waited for; matrix products, arithmetic and copies ran while one was open for 18% of the time, Pallas kernels for 0%

commit v1 on v0

--- a/solution.py
+++ b/solution.py
@@ -76,7 +76,9 @@
     held_seq = lax.dynamic_index_in_dim(block_table, ctx_index, 0, keepdims=False)
     key_store, allowed = slot_layout(block_table, pattern, held_seq)
     key_all, value_all = (
-        lax.all_gather(key_rows, "ctx", axis=0, tiled=True),
+        jnp.concatenate(
+            lax.all_to_all(jnp.stack([key_rows] * lax.axis_size("ctx")), "ctx", 0, 0), axis=0
+        ),
         lax.all_gather(stored_value_rows, "ctx", axis=0, tiled=True),
     )
     key_blocks = key_all.reshape(blocks, BLK, kv_local, HEAD_SIZE)

time: 323 us -> 278 us (0.86)
  waiting for transfers between devices: 249 us -> 191 us
  starting transfers between devices: 0.34 us -> 10.4 us
    all_gather x1 -> x0, waiting for transfers between devices: 54.9 us -> none  [per_device(): lax.all_gather(key_rows, 'ctx', axis=0, tiled=True)]
    all_gather x1, waiting for transfers between devices: 41.2 us -> 24.6 us  [per_device(): lax.all_gather(stored_value_rows, 'ctx', axis=0, tiled=True)]
    all_to_all x0 -> x1, waiting for transfers between devices: none -> 14.5 us  [per_device(): lax.all_to_all(jnp.stack([key_rows] * lax.axis_size('ctx')), 'ctx', 0, 0)]
    all_to_all x0 -> x1, starting transfers between devices: none -> 10.1 us  [per_device(): lax.all_to_all(jnp.stack([key_rows] * lax.axis_size('ctx')), 'ctx', 0, 0)]
  transfers between devices with their start and end apart: 4 -> 4, of which waited for: 4 -> 4; matrix products, arithmetic and copies ran while one was open for 18% -> 21% of each run, Pallas kernels for 0% -> 0%
where the time goes in v1:
time: 278 us; the launch traced here: 277 us
  waiting for transfers between devices  191 us (69%)
  matrix products  21.8 us (8%)
  other arithmetic  20.2 us (7%)
  local copies, waits for them, and re-layouts  20 us (7%)
  between operations  14 us (5%)
  starting transfers between devices  10.4 us (4%)
    reduce_scatter x1, waiting for transfers between devices, per_device(): lax.psum_scatter(key_partial.reshape(blocks * BLK, -1).astype(jnp.bfloat1...  90.3 us
    reduce_scatter x1, waiting for transfers between devices, per_device(): lax.psum_scatter(value_partial.reshape(blocks * BLK, -1).astype(jnp.bfloa...  60.9 us
    all_gather x1, waiting for transfers between devices, per_device(): lax.all_gather(stored_value_rows, 'ctx', axis=0, tiled=True)  24.6 us
    all_to_all x1, waiting for transfers between devices, per_device(): lax.all_to_all(jnp.stack([key_rows] * lax.axis_size('ctx')), 'ctx', 0, 0)  14.5 us
    all_to_all x1, starting transfers between devices, per_device(): lax.all_to_all(jnp.stack([key_rows] * lax.axis_size('ctx')), 'ctx', 0, 0)  10.1 us
    dot_general x1, matrix products, attend_tiles(): jnp.einsum('bagijk,bjkad->biagd', prob_low, value_tiles, preferred_elemen...  7.98 us
    unnamed x26, local copies, waits for them, and re-layouts  6.38 us
    scatter-add x1, other arithmetic, per_device(): value_partial = jnp.zeros((blocks, BLK, kv_local, HEAD_SIZE), jnp.float32...  5.85 us
  transfers between devices with their start and end apart: 4, of which 4 were waited for; matrix products, arithmetic and copies ran while one was open for 21% of the time, Pallas kernels for 0%

profile of v1, /device:TPU:2, one launch (start us, length us, event | category | flops | bytes accessed | tf_op | source)
XLA Modules:
  0.0 277.5 jit_solution(11878013334943655799)
XLA Ops:
  7.2 2.0 stack.2
  9.2 10.1 %all-to-all-start = ((bf16[16,256,128]{2,1,0:T(8,128)(2,1)}), bf16[16,256,128]{2,1,0:T(8,128)(2,1)S(1)}, u32[]{:S(2)}, u32[]{:S(2)}) async-start(bf16[16,256,128]{2,1,0:T(8,128)(2,1)} %stack.2), calls=%async_computation | async-start | bytes 2097152 | tf_op jit(solution)/shard_map/all_to_all | solution.py:80
  26.1 1.9 copy.97
  28.2 1.4 copy.60
  30.4 2.0 bitcast_bitcast_fusion
  32.3 14.5 %all-to-all-done = bf16[16,256,128]{2,1,0:T(8,128)(2,1)S(1)} async-done(((bf16[16,256,128]{2,1,0:T(8,128)(2,1)}), bf16[16,256,128]{2,1,0:T(8,128)(2,1)S(1)}, u32[]{:S(2)}, u32[]{:S(2)}) %all-to-all-start) | async-done | bytes 1048608 | tf_op jit(solution)/shard_map/all_to_all | solution.py:80
  47.5 1.5 fusion.4
  49.1 2.3 exponential_reduce_fusion
  51.4 2.5 fusion.9
  53.9 1.5 broadcast.136.clone.1
  55.5 5.8 %scatter_fusion.1 = f32[32,128,128]{2,1,0:T(8,128)} fusion(f32[32,128,128]{2,1,0:T(8,128)} %broadcast.136.clone.1, s32[20]{0:T(128)S(1)} %fusion.17, f32[20,128,128]{2,1,0:T(8,128)S(1)} %bitcast.167), kind=kCustom, calls=%fused_computation.3 | custom fusion | flops 327680 | bytes 3932240 | tf_op jit(solution)/shard_map/scatter-add | solution.py:102
  61.3 3.0 %convert_element_type.70 = bf16[32,128,128]{2,1,0:T(8,128)(2,1)} convert(f32[32,128,128]{2,1,0:T(8,128)} %scatter_fusion.1) | non-fusion elementwise | flops 524288 | bytes 3145728 | tf_op jit(solution)/shard_map/convert_element_type | solution.py:112
  64.6 24.6 %all-gather.2.cloned.1.call-done = bf16[4096,128]{1,0:T(8,128)(2,1)} async-done(((bf16[256,128]{1,0:T(8,128)(2,1)}), bf16[4096,128]{1,0:T(8,128)(2,1)}) %all-gather.2.cloned.1.call-update) | async-done | bytes 1048592 | tf_op jit(solution)/shard_map/all_gather | solution.py:82
  89.2 2.8 gather_fusion
  91.9 8.0 %multiply_reduce_fusion = (f32[2,128,8]{1,2,0:T(8,128)S(1)}, bf16[2,128,1,8,128]{1,4,3,0,2:T(8,128)(2,1)}) fusion(f32[2,128,1,8,128]{1,4,3,0,2:T(8,128)} %copy.60, bf16[2,10,128,128,1]{3,2,4,1,0:T(8,128)(2,1)} %bitcast.168, f32[2,10,128,128,8]{3,2,4,1,0:T(8,128)} %copy-done, f32[2,8,128]{2,1,0:T(8,128)S(1)} %log_add_fusion, ...), kind=kOutput, calls=%fused_computation.21 | convolution fusion | flops 682358784 | bytes 13058048 | tf_op jit(solution)/shard_map/bagijk,bjkad->biagd/dot_general | solution.py:47
  100.0 3.6 %fusion.6 = bf16[2,8,128,10,128]{2,4,1,3,0:T(8,128)(2,1)S(1)} fusion(f32[2,10,128,128,8]{3,2,4,1,0:T(8,128)S(1)} %bitcast.154, f32[2,8,128]{2,1,0:T(8,128)S(1)} %bitcast.172, f32[2,8,128]{2,1,0:T(8,128)S(1)} %log_add_fusion, pred[2,128,10,128]{1,3,2,0:T(8,128)(4,1)S(1)} %copy-done.3, bf16[2,10,128,128,1]{3,2,4,1,0:T(8,128)(2,1)S(1)} %bitcast.169, ...), kind=kOutput, calls=%fused_computation.14 | convolution fusion | flops 689438720 | bytes 17252352 | tf_op jit(solution)/shard_map/biagd,bjkad->bagijk/dot_general | solution.py:53
  103.6 2.3 copy-done.1
  105.9 2.6 fusion.12
  108.8 4.4 %scatter_fusion = f32[32,128,128]{2,1,0:T(8,128)S(1)} fusion(f32[32,128,128]{2,1,0:T(8,128)S(1)} %broadcast.136.clone, s32[20]{0:T(128)S(1)} %fusion.17, f32[20,128,128]{2,1,0:T(8,128)} %bitcast.157), kind=kCustom, calls=%fused_computation.2 | custom fusion | flops 327680 | bytes 3932240 | tf_op jit(solution)/shard_map/scatter-add | solution.py:97
  113.2 1.2 convert_element_type.69
  114.4 3.5 %fusion.8 = bf16[2,128,1,8,128]{1,4,3,0,2:T(8,128)(2,1)S(1)} fusion(bf16[2,10,128,128,1]{3,2,4,1,0:T(8,128)(2,1)S(1)} %bitcast.156, bf16[2,8,128,10,128]{2,4,1,3,0:T(8,128)(2,1)} %copy-done.1), kind=kOutput, calls=%fused_computation.19 | convolution fusion | flops 671350784 | bytes 6422528 | tf_op jit(solution)/shard_map/bagijk,bjkad->biagd/dot_general | solution.py:57
  118.5 1.2 copy_bitcast_fusion
  119.7 60.9 %reduce-scatter.5.cloned.1.call-done = bf16[256,128]{1,0:T(8,128)(2,1)} async-done(((bf16[4096,128]{1,0:T(8,128)(2,1)}), bf16[256,128]{1,0:T(8,128)(2,1)}) %reduce-scatter.5.cloned.1.call-update) | async-done | bytes 65552 | tf_op jit(solution)/shard_map/reduce_scatter | solution.py:111
  180.6 90.3 %reduce-scatter.3.cloned.1.call-done = bf16[256,128]{1,0:T(8,128)(2,1)} async-done(((bf16[4096,128]{1,0:T(8,128)(2,1)}), bf16[256,128]{1,0:T(8,128)(2,1)}) %reduce-scatter.3.cloned.1.call-update) | async-done | bytes 65552 | tf_op jit(solution)/shard_map/reduce_scatter | solution.py:105
  (59 shorter events, 9.5 us)
Async XLA Ops:
  9.2 37.6 %all-to-all-start = ((bf16[16,256,128]{2,1,0:T(8,128)(2,1)}), bf16[16,256,128]{2,1,0:T(8,128)(2,1)S(1)}, u32[]{:S(2)}, u32[]{:S(2)}) async-start(bf16[16,256,128]{2,1,0:T(8,128)(2,1)} %stack.2), calls=%async_computation | async-start | bytes 2097152 | tf_op jit(solution)/shard_map/all_to_all | solution.py:80
  19.3 69.9 %all-gather.2.cloned.1.call-start = ((), (), s32[]{:S(2)}) async-start(), calls=%async_computation.3 | async-start | bytes 1114112 | tf_op jit(solution)/shard_map/all_gather | solution.py:82
  20.0 160.6 %reduce-scatter.5.cloned.1.call-start = ((), (), s32[]{:S(2)}) async-start(), calls=%async_computation.5 | async-start | bytes 1114112 | tf_op jit(solution)/shard_map/reduce_scatter | solution.py:111
  30.3 25.2 %copy-start.2 = (pred[2,128,10,128]{1,3,2,0:T(8,128)(4,1)}, pred[2,128,10,128]{1,3,2,0:T(8,128)(4,1)S(1)}, u32[]{:S(2)}) copy-start(pred[2,128,10,128]{1,3,2,0:T(8,128)(4,1)S(1)} %compare_and_fusion) | copy-start | bytes 983044
  47.5 3.9 %copy-start.5 = (bf16[2,128,8,128,1]{3,2,1,0,4:T(8,128)(2,1)S(1)}, bf16[2,128,8,128,1]{3,2,1,0,4:T(8,128)(2,1)}, u32[]{:S(2)}) copy-start(bf16[2,128,8,128,1]{3,2,1,0,4:T(8,128)(2,1)} %bitcast_bitcast_fusion) | copy-start | bytes 1572868
  49.1 4.9 %copy-start = (f32[2,10,128,128,8]{3,2,4,1,0:T(8,128)}, f32[2,10,128,128,8]{3,2,4,1,0:T(8,128)S(1)}, u32[]{:S(2)}) copy-start(f32[2,10,128,128,8]{3,2,4,1,0:T(8,128)S(1)} %get-tuple-element.7) | copy-start | bytes 31457284
  61.3 38.6 %slice-start = ((s8[10485760]{0:T(1024)(128)(4,1)}), s8[2097152]{0:T(1024)(128)(4,1)S(1)}, s32[]{:S(2)}) async-start(s8[10485760]{0:T(1024)(128)(4,1)} %bitcast.153), calls=%async_computation.6 | async-start | bytes 4194304
  64.3 206.6 %reduce-scatter.3.cloned.1.call-start = ((), (), s32[]{:S(2)}) async-start(), calls=%async_computation.4 | async-start | bytes 1114112 | tf_op jit(solution)/shard_map/reduce_scatter | solution.py:105
  91.9 8.0 %copy-start.3 = (pred[2,128,10,128]{1,3,2,0:T(8,128)(4,1)S(1)}, pred[2,128,10,128]{1,3,2,0:T(8,128)(4,1)}, u32[]{:S(2)}) copy-start(pred[2,128,10,128]{1,3,2,0:T(8,128)(4,1)} %copy-done.2) | copy-start | bytes 983044
  91.9 8.0 %copy-start.4 = (bf16[20,128,128]{2,1,0:T(8,128)(2,1)S(1)}, bf16[20,128,128]{2,1,0:T(8,128)(2,1)}, u32[]{:S(2)}) copy-start(bf16[20,128,128]{2,1,0:T(8,128)(2,1)} %gather_fusion) | copy-start | bytes 1966084
  91.9 8.0 %copy-start.6 = (bf16[2,128,8,128,1]{3,2,1,0,4:T(8,128)(2,1)S(1)}, bf16[2,128,8,128,1]{3,2,1,0,4:T(8,128)(2,1)}, u32[]{:S(2)}) copy-start(bf16[2,128,8,128,1]{3,2,1,0,4:T(8,128)(2,1)} %bitcast_bitcast_fusion) | copy-start | bytes 1572868
  91.9 8.0 %slice-start.1 = ((s8[10485760]{0:T(1024)(128)(4,1)}), s8[4194304]{0:T(1024)(128)(4,1)S(1)}, s32[]{:S(2)}) async-start(s8[10485760]{0:T(1024)(128)(4,1)} %bitcast.153), calls=%async_computation.7 | async-start | bytes 8388608
  91.9 8.0 %slice-start.2 = ((s8[10485760]{0:T(1024)(128)(4,1)}), s8[4194304]{0:T(1024)(128)(4,1)S(1)}, s32[]{:S(2)}) async-start(s8[10485760]{0:T(1024)(128)(4,1)} %bitcast.153), calls=%async_computation.8 | async-start | bytes 8388608
  103.6 2.3 copy-start.1
  108.5 9.7 %copy-start.7 = (bf16[2,128,1,8,128]{1,4,3,0,2:T(8,128)(2,1)S(1)}, bf16[2,128,1,8,128]{1,4,3,0,2:T(8,128)(2,1)}, u32[]{:S(2)}) copy-start(bf16[2,128,1,8,128]{1,4,3,0,2:T(8,128)(2,1)} %get-tuple-element.5) | copy-start | bytes 1572868
Sparse Core Ops, SparseCore 0:
  23.4 65.7 all-gather.1
  94.4 86.1 reduce-scatter.4
  186.6 84.2 reduce-scatter.2
